TPU v7x, 32 devices: a whole 2x2x4 slice. The times are simulated.
32 devices in a mesh: dp: 8 (over z, x), tensor: 4 (over y, core).
Axes of the slice: x: 2, y: 2, z: 4, core: 2. Of those that a mesh axis runs over, the one named last changes fastest.
Arguments:
- bag_items: bfloat16 [16384, 64, 128], P('dp', 'tensor'), may hold values from -1.1953125 to 1.1953125
- bag_lengths: int32 [2048, 64], P('dp', 'tensor'), may hold values from 0 to 16, as said below
- send_counts: int32 [8, 8], P('dp'), may hold values from 0 to 48, as said below
- cross_weight: bfloat16 [1, 8192, 8192], P(None, 'tensor', 'dp'), may hold values from -0.0625 to 0.0625
- cross_bias: float32 [1, 8192], P(None, 'tensor'), may hold values from -3 to 3
Outputs:
- crossed: bfloat16 [2048, 8192], P('dp', 'tensor')
Inputs may be any that keep to these rules, and one draw needn't show every extreme that they name: `bag_lengths`: for every feature, the bags of the 256 rows of one aligned block hold 2048 items together; bags may be empty; in every aligned block and feature some bag holds exactly 16 items. `send_counts`: every row and every column sums to 256; each row has eight nonzero entries, one of them may be on the diagonal; no entry exceeds 48 and every row has an entry equal to 48.
All inputs are finite; a program needn't handle non-finite values.
Results may differ from a plain program's by a relative error of at most 0.0053.
Values may be sent and summed in bfloat16 or wider, within the bound.
No kernel may reach another device: no remote copies, remote signals or barrier semaphores. Data moves between devices by JAX's collectives and lax.ppermute only.
A program may use at most 128 MiB of HBM per device.

v0:
```python
import jax
import jax.numpy as jnp
from jax import lax
from jax.sharding import PartitionSpec as P

BAG = 8
CAP = 48


def shards(bag_items, bag_lengths, send_counts, cross_weight, cross_bias):
    row_count = bag_lengths.shape[0]
    feat_count = bag_lengths.shape[1]
    slot_count = bag_items.shape[0]
    embed_width = bag_items.shape[2]
    block_width = feat_count * embed_width
    bag_ends = jnp.cumsum(bag_lengths, axis=0)
    bag_starts = bag_ends - bag_lengths
    row_block = min(128, row_count)
    block_total = row_count // row_block
    window = min(slot_count, 2 * BAG * row_block)
    first_starts = bag_starts.reshape(block_total, row_block, feat_count)[:, 0, :]
    window_starts = jnp.clip(first_starts, 0, slot_count - window)
    feature_ids = jnp.arange(feat_count, dtype=jnp.int32)

    def take_window(start, feature):
        piece = lax.dynamic_slice(
            bag_items, (start, feature, jnp.int32(0)), (window, 1, embed_width)
        )
        return piece[:, 0, :]

    def pool_block(block_id):
        starts = window_starts[block_id]
        window_items = jax.vmap(take_window)(starts, feature_ids)
        row_first = (
            lax.dynamic_slice_in_dim(bag_starts, block_id * row_block, row_block, 0)
            - starts[None, :]
        )
        row_last = (
            lax.dynamic_slice_in_dim(bag_ends, block_id * row_block, row_block, 0) - starts[None, :]
        )
        positions = lax.broadcasted_iota(jnp.int32, (feat_count, row_block, window), 2)
        member = (positions >= row_first.T[:, :, None]) & (positions < row_last.T[:, :, None])
        one_hot = member.astype(jnp.bfloat16)
        return jnp.einsum("frs,fse->rfe", one_hot, window_items, preferred_element_type=jnp.float32)

    pooled_sum = lax.map(pool_block, jnp.arange(block_total, dtype=jnp.int32))
    pooled = pooled_sum.reshape(row_count, block_width).astype(jnp.bfloat16)
    device_count = lax.axis_size("dp")
    count_row = send_counts.reshape(-1)
    send_end = jnp.cumsum(count_row)
    send_start = send_end - count_row
    slot_ids = jnp.arange(CAP, dtype=jnp.int32)
    slot_index = jnp.minimum(send_start[:, None] + slot_ids[None, :], row_count - 1)
    slot_valid = slot_ids[None, :] < count_row[:, None]
    outgoing = jnp.where(slot_valid[:, :, None], pooled[slot_index], jnp.zeros((), jnp.bfloat16))
    received, recv_column = (
        lax.all_to_all(outgoing, "dp", split_axis=0, concat_axis=0, tiled=True),
        lax.all_to_all(
            count_row.reshape(device_count, 1), "dp", split_axis=0, concat_axis=0, tiled=True
        ),
    )
    recv_counts = recv_column.reshape(-1)
    recv_end = jnp.cumsum(recv_counts).astype(jnp.int32)
    recv_start = recv_end - recv_counts
    target_rows = jnp.arange(row_count, dtype=jnp.int32)
    source_block = jnp.sum((recv_end[None, :] <= target_rows[:, None]).astype(jnp.int32), axis=1)
    source_match = jnp.arange(device_count, dtype=jnp.int32)[None, :] == source_block[:, None]
    source_start = jnp.sum(jnp.where(source_match, recv_start[None, :], 0), axis=1)
    flat_index = source_block * CAP + target_rows - source_start
    cross_input = received.reshape(device_count * CAP, block_width)[flat_index]
    base_rows = cross_input.astype(jnp.float32)
    state = cross_input
    gathered = lax.all_gather(state, "tensor", axis=1, tiled=True)
    layer_weight = cross_weight[0]
    empty_sum = jnp.zeros((row_count, block_width), jnp.float32)
    w_piece = lax.all_gather(layer_weight, "dp", axis=1, tiled=True)
    columns = lax.slice_in_dim(gathered, 0, w_piece.shape[1], axis=1)
    product = empty_sum + lax.dot_general(
        columns, w_piece, (((1,), (1,)), ((), ())), preferred_element_type=jnp.float32
    )
    state = (base_rows * (product + cross_bias[0]) + state.astype(jnp.float32)).astype(jnp.bfloat16)
    return state


def solution(mesh):
    return jax.shard_map(
        shards,
        mesh=mesh,
        in_specs=(
            P("dp", "tensor", None),
            P("dp", "tensor"),
            P("dp", None),
            P(None, "tensor", "dp"),
            P(None, "tensor"),
        ),
        out_specs=P("dp", "tensor"),
        check_vma=False,
    )
```

profile of v0, /device:TPU:0, one launch (start us, length us, event | category | flops | bytes accessed | tf_op | source)
XLA Modules:
  0.0 814.9 jit_solution(1087858234139182849)
XLA Ops:
  6.5 1.3 copy.32
  7.9 7.3 all-to-all-start.1
  15.1 0.7 copy_bitcast_fusion.1
  15.8 0.6 reduce-window.25
  16.4 0.2 slice_reduce_fusion
  16.6 0.8 fusion.29
  17.4 0.1 bitcast_bitcast_fusion
  17.5 0.1 copy.33
  17.6 12.3 %copy.30 = bf16[2048,16,128]{0,2,1:T(8,128)(2,1)} copy(bf16[2048,16,128]{2,1,0:T(8,128)(2,1)} %param.7) | data formatting | bytes 16777216
  29.9 37.9 %while.11 = (s32[]{:T(128)}, bf16[2,128,16,128]{1,3,2,0:T(8,128)(2,1)S(1)}, s32[2]{0:T(128)S(1)}, s32[2,16]{1,0:T(2,128)S(1)}, bf16[2048,16,128]{0,2,1:T(8,128)(...) while((s32[]{:T(128)}, ...), condition=%wide.region_3.4_spmd.clone, body=%wide.region_2.3_spmd.clone.sunk | while | flops 1086328960 | bytes 26264288 | solution.py:46
  29.9 0.6 dynamic_slice.31
  32.8 0.1 subtract_bitcast_fusion.3
  32.9 8.3 %gather_fusion = bf16[16,2048,128]{1,2,0:T(8,128)(2,1)} fusion(bf16[2048,16,128]{0,2,1:T(8,128)(2,1)} %get-tuple-element.190, s32[16]{0:T(128)S(1)} %fusion.40), kind=kCustom, calls=%fused_computation.clone.clone.1 | custom fusion | bytes 16777408 | tf_op jit(solution)/shard_map/while/body/eval_jaxpr/vmap()/gather | solution.py:26
  41.1 7.8 fusion.42
  48.9 0.6 dynamic_slice.31
  51.8 0.1 subtract_bitcast_fusion.3
  51.9 8.3 %gather_fusion = bf16[16,2048,128]{1,2,0:T(8,128)(2,1)} fusion(bf16[2048,16,128]{0,2,1:T(8,128)(2,1)} %get-tuple-element.190, s32[16]{0:T(128)S(1)} %fusion.40), kind=kCustom, calls=%fused_computation.clone.clone.1 | custom fusion | bytes 16777408 | tf_op jit(solution)/shard_map/while/body/eval_jaxpr/vmap()/gather | solution.py:26
  60.1 7.8 fusion.42
  67.9 0.0 copy-start.1
  67.9 1.0 copy.31
  68.9 0.3 copy.42
  69.1 0.0 copy-done.1
  69.2 0.2 reduce-window.27
  69.3 0.1 compare_select_fusion.1
  69.4 0.1 reshape.249
  69.5 0.1 iota_compare_fusion.5
  69.6 2.4 gather_fusion.1
  72.0 1.3 broadcast_select_fusion
  73.4 0.0 all-to-all-done.1
  73.4 6.0 all-to-all-start
  79.4 0.0 all-gather.5.cloned.1.call-start
  79.4 0.2 reduce.1
  79.7 0.2 reduce-window.28
  79.8 0.1 convert_reduce_fusion
  79.9 0.1 select_reduce_fusion
  80.0 35.8 %all-to-all-done = bf16[8,48,2048]{2,1,0:T(8,128)(2,1)S(1)} async-done(((bf16[8,48,2048]{2,1,0:T(8,128)(2,1)}), bf16[8,48,2048]{2,1,0:T(8,128)(2,1)S(1)}, u32[]{:S(2)}, u32[]{:S(2)}) %all-to-all-start) | async-done | bytes 1572896 | tf_op jit(solution)/shard_map/all_to_all | solution.py:57
  115.8 2.3 gather_fusion.2
  118.1 0.0 copy-start
  118.1 0.0 copy-start.2
  118.1 0.0 all-gather.5.cloned.1.call-update
  118.2 0.0 all-gather.7.cloned.1.call-start
  118.2 0.7 all-gather.7.cloned.1.call-update
  118.9 33.0 %all-gather.5.cloned.1.call-done = bf16[256,8192]{1,0:T(8,128)(2,1)} async-done(((bf16[256,2048]{1,0:T(8,128)(2,1)}), bf16[256,8192]{1,0:T(8,128)(2,1)}) %all-gather.5.cloned.1.call-update) | async-done | bytes 4194320 | tf_op jit(solution)/shard_map/all_gather | solution.py:73
  151.9 639.3 %all-gather.7.cloned.1.call-done = bf16[1,2048,8192]{2,1,0:T(8,128)(2,1)} async-done(((bf16[1,2048,1024]{2,1,0:T(8,128)(2,1)}), bf16[1,2048,8192]{2,1,0:T(8,128)(2,1)}) %all-gather.7.cloned.1.call-update) | async-done | bytes 33554448 | tf_op jit(solution)/shard_map/all_gather | solution.py:76
  791.2 0.0 copy-done
  791.2 0.0 copy-done.2
  791.2 16.8 %fusion.26 = bf16[256,2048]{1,0:T(8,128)(2,1)} fusion(bf16[256,8192]{1,0:T(8,128)(2,1)} %all-gather.5.cloned.1.call-done, bf16[1,2048,8192]{2,1,0:T(8,128)(2,1)} %all-gather.7.cloned.1.call-done, bf16[256,2048]{1,0:T(8,128)(2,1)S(1)} %copy-done, f32[2048]{0:T(1024)S(1)} %bitcast.99), kind=kOutput, calls=%fused_computation.27 | convolution fusion | flops 8592556032 | bytes 39854080 | tf_op jit(solution)/shard_map/dot_general | solution.py:78
  (16 shorter events, 0.1 us)
Async XLA Ops:
  7.9 65.5 %all-to-all-start.1 = ((s32[8,1,1]{2,1,0:T(1,128)}), s32[8,1,1]{2,1,0:T(1,128)S(1)}, u32[]{:S(2)}, u32[]{:S(2)}) async-start(s32[8,1,1]{2,1,0:T(1,128)} %copy.32), calls=%async_computation.1 | async-start | bytes 8192 | tf_op jit(solution)/shard_map/all_to_all | solution.py:58
  67.9 1.3 copy-start.1
  73.4 42.4 %all-to-all-start = ((bf16[8,48,2048]{2,1,0:T(8,128)(2,1)}), bf16[8,48,2048]{2,1,0:T(8,128)(2,1)S(1)}, u32[]{:S(2)}, u32[]{:S(2)}) async-start(bf16[8,48,2048]{2,1,0:T(8,128)(2,1)} %broadcast_select_fusion), calls=%async_computation | async-start | bytes 3145728 | tf_op jit(solution)/shard_map/all_to_all | solution.py:57
  79.4 72.5 %all-gather.5.cloned.1.call-start = ((), (), s32[]{:S(2)}) async-start(), calls=%async_computation.2 | async-start | bytes 5242880 | tf_op jit(solution)/shard_map/all_gather | solution.py:73
  118.1 673.1 %copy-start = (bf16[256,2048]{1,0:T(8,128)(2,1)S(1)}, bf16[256,2048]{1,0:T(8,128)(2,1)}, u32[]{:S(2)}) copy-start(bf16[256,2048]{1,0:T(8,128)(2,1)} %gather_fusion.2) | copy-start | bytes 3145732
  118.1 673.1 %copy-start.2 = (f32[1,2048]{1,0:T(1,128)S(1)}, f32[1,2048]{1,0:T(1,128)}, u32[]{:S(2)}) copy-start(f32[1,2048]{1,0:T(1,128)} %param.11) | copy-start | bytes 24580
  118.2 673.0 %all-gather.7.cloned.1.call-start = ((), (), s32[]{:S(2)}) async-start(), calls=%async_computation.3 | async-start | bytes 37748736 | tf_op jit(solution)/shard_map/all_gather | solution.py:76
Sparse Core Ops, SparseCore 0:
  118.3 33.5 all-gather.4
  153.4 637.7 all-gather.6
where the time goes:
time: 816 us; the launch traced here: 815 us
  waiting for transfers between devices  709 us (87%)
  local copies, waits for them, and re-layouts  38.4 us (5%)
  matrix products  32.3 us (4%)
  between operations  13.5 us (2%)
  starting transfers between devices  13.3 us (2%)
    all_gather x1, waiting for transfers between devices, shards(): w_piece = lax.all_gather(layer_weight, 'dp', axis=1, tiled=True)  639 us
    all_to_all x1, waiting for transfers between devices, shards(): lax.all_to_all(outgoing, 'dp', split_axis=0, concat_axis=0, tiled=True)  35.8 us
    all_gather x1, waiting for transfers between devices, shards(): gathered = lax.all_gather(state, 'tensor', axis=1, tiled=True)  33 us
    dot_general x1, matrix products, shards(): lax.dot_general(columns, w_piece, (((1,), (1,)), ((), ())), preferred_ele...  16.8 us
    gather x2, local copies, waits for them, and re-layouts, take_window(): lax.dynamic_slice(bag_items, (start, feature, jnp.int32(0)), (window, 1,...  16.5 us
  transfers between devices with their start and end apart: 4, of which 3 were waited for; matrix products, arithmetic and copies ran while one was open for 7% of the time, Pallas kernels for 0%

commit v1 on v0

--- a/solution.py
+++ b/solution.py
@@ -73,7 +73,13 @@
     gathered = lax.all_gather(state, "tensor", axis=1, tiled=True)
     layer_weight = cross_weight[0]
     empty_sum = jnp.zeros((row_count, block_width), jnp.float32)
-    w_piece = lax.all_gather(layer_weight, "dp", axis=1, tiled=True)
+    count = lax.axis_size("dp")
+    held, parts = (layer_weight, [layer_weight])
+    for _ in range(count - 1):
+        held = lax.ppermute(held, "dp", [(i, (i + 1) % count) for i in range(count)])
+        parts.insert(0, held)
+    merged = jnp.concatenate(parts, axis=1)
+    w_piece = jnp.roll(merged, (lax.axis_index("dp") + 1) * layer_weight.shape[1], axis=1)
     columns = lax.slice_in_dim(gathered, 0, w_piece.shape[1], axis=1)
     product = empty_sum + lax.dot_general(
         columns, w_piece, (((1,), (1,)), ((), ())), preferred_element_type=jnp.float32

time: 816 us -> 776 us (0.951); the launches traced: 815 us -> 767 us
  waiting for transfers between devices: 709 us -> 598 us
  local copies, waits for them, and re-layouts: 38.4 us -> 98.6 us
    all_gather x1 -> x0, waiting for transfers between devices: 639 us -> none  [shards(): w_piece = lax.all_gather(layer_weight, 'dp', axis=1, tiled=True)]
    ppermute x0 -> x7, waiting for transfers between devices: none -> 496 us  [shards(): lax.ppermute(held, 'dp', [(i, (i + 1) % count) for i in range(count)])]
    all_to_all x1, waiting for transfers between devices: 35.8 us -> 101 us  [shards(): lax.all_to_all(outgoing, 'dp', split_axis=0, concat_axis=0, tiled=True)]
    unnamed x9 -> x42, local copies, waits for them, and re-layouts: 12.7 us -> 70.4 us
    all_gather x1, waiting for transfers between devices: 33 us -> 0.01 us  [shards(): gathered = lax.all_gather(state, 'tensor', axis=1, tiled=True)]
  transfers between devices with their start and end apart: 4 -> 10, of which waited for: 3 -> 7; matrix products, arithmetic and copies ran while one was open for 7% -> 14% of each run, Pallas kernels for 0% -> 0%
where the time goes in v1:
time: 776 us; the launch traced here: 767 us
  waiting for transfers between devices  598 us (77%)
  local copies, waits for them, and re-layouts  98.6 us (13%)
  matrix products  32.6 us (4%)
  starting transfers between devices  15.2 us (2%)
  between operations  13.5 us (2%)
    ppermute x7, waiting for transfers between devices, shards(): lax.ppermute(held, 'dp', [(i, (i + 1) % count) for i in range(count)])  496 us
    all_to_all x1, waiting for transfers between devices, shards(): lax.all_to_all(outgoing, 'dp', split_axis=0, concat_axis=0, tiled=True)  101 us
    unnamed x42, local copies, waits for them, and re-layouts  70.4 us
    dot_general x1, matrix products, shards(): lax.dot_general(columns, w_piece, (((1,), (1,)), ((), ())), preferred_ele...  17.1 us
    gather x2, local copies, waits for them, and re-layouts, take_window(): lax.dynamic_slice(bag_items, (start, feature, jnp.int32(0)), (window, 1,...  16.5 us
  transfers between devices with their start and end apart: 10, of which 7 were waited for; matrix products, arithmetic and copies ran while one was open for 14% of the time, Pallas kernels for 0%

profile of v1, /device:TPU:0, one launch (start us, length us, event | category | flops | bytes accessed | tf_op | source)
XLA Modules:
  0.0 766.5 jit_solution(3271563085243722938)
XLA Ops:
  6.5 2.9 collective-permute-start
  9.5 93.8 %collective-permute-done = bf16[2048,1024]{1,0:T(8,128)(2,1)S(1)} collective-permute-done((bf16[2048,1024]{1,0:T(8,128)(2,1)}, bf16[2048,1024]{1,0:T(8,128)(2,1)S(1)}, u32[]{:S(2)}, u32[]{:S(2)}) %collective-permute-start) | collective-permute-done | bytes 4194336 | tf_op jit(solution)/shard_map/ppermute | solution.py:79
  103.3 2.0 copy-done.1
  105.3 94.5 %collective-permute-done.1 = bf16[2048,1024]{1,0:T(8,128)(2,1)S(1)} collective-permute-done((bf16[2048,1024]{1,0:T(8,128)(2,1)S(1)}, bf16[2048,1024]{1,0:T(8,128)(2,1)S(1)}, u32[]{:S(2)}, u32[]{:S(2)}) %collective-permute-start.1) | collective-permute-done | bytes 4194336 | tf_op jit(solution)/shard_map/ppermute | solution.py:79
  199.7 2.0 copy-done.3
  201.7 93.5 %collective-permute-done.2 = bf16[2048,1024]{1,0:T(8,128)(2,1)S(1)} collective-permute-done((bf16[2048,1024]{1,0:T(8,128)(2,1)S(1)}, bf16[2048,1024]{1,0:T(8,128)(2,1)S(1)}, u32[]{:S(2)}, u32[]{:S(2)}) %collective-permute-start.2) | collective-permute-done | bytes 4194336 | tf_op jit(solution)/shard_map/ppermute | solution.py:79
  295.3 1.9 copy-done.5
  297.2 92.6 %collective-permute-done.3 = bf16[2048,1024]{1,0:T(8,128)(2,1)S(1)} collective-permute-done((bf16[2048,1024]{1,0:T(8,128)(2,1)S(1)}, bf16[2048,1024]{1,0:T(8,128)(2,1)S(1)}, u32[]{:S(2)}, u32[]{:S(2)}) %collective-permute-start.3) | collective-permute-done | bytes 4194336 | tf_op jit(solution)/shard_map/ppermute | solution.py:79
  389.8 2.0 copy-done.7
  391.8 91.8 %collective-permute-done.4 = bf16[2048,1024]{1,0:T(8,128)(2,1)} collective-permute-done((bf16[2048,1024]{1,0:T(8,128)(2,1)S(1)}, bf16[2048,1024]{1,0:T(8,128)(2,1)}, u32[]{:S(2)}, u32[]{:S(2)}) %collective-permute-start.4) | collective-permute-done | bytes 4194336 | tf_op jit(solution)/shard_map/ppermute | solution.py:79
  483.6 1.3 copy.32
  484.9 6.0 all-to-all-start.1
  490.9 0.7 copy_bitcast_fusion.1
  491.6 0.6 reduce-window.25
  492.4 0.8 fusion.30
  493.3 12.4 %copy.30 = bf16[2048,16,128]{0,2,1:T(8,128)(2,1)} copy(bf16[2048,16,128]{2,1,0:T(8,128)(2,1)} %param.7) | data formatting | bytes 16777216
  506.0 38.5 %while.11 = (s32[]{:T(128)}, bf16[2,128,16,128]{1,3,2,0:T(8,128)(2,1)S(1)}, s32[2]{0:T(128)S(1)}, s32[2,16]{1,0:T(2,128)S(1)}, bf16[2048,16,128]{0,2,1:T(8,128)(...) while((s32[]{:T(128)}, ...), condition=%wide.region_3.4_spmd.clone, body=%wide.region_2.3_spmd.clone.sunk | while | flops 1086328960 | bytes 26264288 | solution.py:46
  506.0 0.6 dynamic_slice.44
  509.2 8.3 %gather_fusion = bf16[16,2048,128]{1,2,0:T(8,128)(2,1)} fusion(bf16[2048,16,128]{0,2,1:T(8,128)(2,1)} %get-tuple-element.190, s32[16]{0:T(128)S(1)} %fusion.41), kind=kCustom, calls=%fused_computation.clone.clone.1 | custom fusion | bytes 16777408 | tf_op jit(solution)/shard_map/while/body/eval_jaxpr/vmap()/gather | solution.py:26
  517.5 7.8 %fusion.43 = bf16[2,128,16,128]{1,3,2,0:T(8,128)(2,1)S(1)} fusion(bf16[2,128,16,128]{1,3,2,0:T(8,128)(2,1)S(1)} %get-tuple-element.175, s32[]{:T(128)} %get-tuple-element.174, bf16[16,2048,128]{1,2,0:T(8,128)(2,1)} %gather_fusion, s32[16,128]{1,0:T(8,128)S(1)} %get-tuple-element.160, s32[16,128]{1,0:T(8,128)S(1)} %get-tuple-element.161), kind=kOutput, calls=%fused_computation.11.clone.1 | convolution fusion | flops 1086324736 | bytes 9453572 | tf_op jit(solution)/shard_map/while/body/eval_jaxpr/frs,fse->rfe/dot_general | solution.py:44
  525.3 0.6 dynamic_slice.44
  528.5 8.3 %gather_fusion = bf16[16,2048,128]{1,2,0:T(8,128)(2,1)} fusion(bf16[2048,16,128]{0,2,1:T(8,128)(2,1)} %get-tuple-element.190, s32[16]{0:T(128)S(1)} %fusion.41), kind=kCustom, calls=%fused_computation.clone.clone.1 | custom fusion | bytes 16777408 | tf_op jit(solution)/shard_map/while/body/eval_jaxpr/vmap()/gather | solution.py:26
  536.7 7.8 %fusion.43 = bf16[2,128,16,128]{1,3,2,0:T(8,128)(2,1)S(1)} fusion(bf16[2,128,16,128]{1,3,2,0:T(8,128)(2,1)S(1)} %get-tuple-element.175, s32[]{:T(128)} %get-tuple-element.174, bf16[16,2048,128]{1,2,0:T(8,128)(2,1)} %gather_fusion, s32[16,128]{1,0:T(8,128)S(1)} %get-tuple-element.160, s32[16,128]{1,0:T(8,128)S(1)} %get-tuple-element.161), kind=kOutput, calls=%fused_computation.11.clone.1 | convolution fusion | flops 1086324736 | bytes 9453572 | tf_op jit(solution)/shard_map/while/body/eval_jaxpr/frs,fse->rfe/dot_general | solution.py:44
  544.5 30.2 %collective-permute-done.5 = bf16[2048,1024]{1,0:T(8,128)(2,1)} collective-permute-done((bf16[2048,1024]{1,0:T(8,128)(2,1)}, bf16[2048,1024]{1,0:T(8,128)(2,1)}, u32[]{:S(2)}, u32[]{:S(2)}) %collective-permute-start.5) | collective-permute-done | bytes 4194336 | tf_op jit(solution)/shard_map/ppermute | solution.py:79
  574.7 1.0 copy.31
  575.7 0.3 copy.42
  576.2 2.5 gather_fusion.1
  578.7 1.4 broadcast_select_fusion
  580.1 6.0 all-to-all-start
  587.0 101.1 %all-to-all-done = bf16[8,48,2048]{2,1,0:T(8,128)(2,1)S(1)} async-done(((bf16[8,48,2048]{2,1,0:T(8,128)(2,1)}), bf16[8,48,2048]{2,1,0:T(8,128)(2,1)S(1)}, u32[]{:S(2)}, u32[]{:S(2)}) %all-to-all-start) | async-done | bytes 1572896 | tf_op jit(solution)/shard_map/all_to_all | solution.py:57
  688.0 2.3 gather_fusion.2
  690.4 4.5 constant_dynamic-update-slice_fusion.15
  694.9 4.7 constant_dynamic-update-slice_fusion.14
  699.7 4.7 constant_dynamic-update-slice_fusion.13
  704.4 2.7 constant_dynamic-update-slice_fusion.12
  707.0 2.6 constant_dynamic-update-slice_fusion.11
  709.6 2.6 constant_dynamic-update-slice_fusion.10
  712.2 2.4 constant_dynamic-update-slice_fusion.9
  714.6 2.4 constant_dynamic-update-slice_fusion.8
  717.0 4.5 constant_dynamic-update-slice_fusion.7
  721.5 4.6 constant_dynamic-update-slice_fusion.6
  726.1 4.6 constant_dynamic-update-slice_fusion.5
  730.7 2.4 constant_dynamic-update-slice_fusion.4
  733.1 2.4 constant_dynamic-update-slice_fusion.3
  735.4 2.4 constant_dynamic-update-slice_fusion.2
  737.8 2.4 constant_dynamic-update-slice_fusion.1
  740.2 2.4 constant_dynamic-update-slice_fusion
  742.5 17.1 %fusion.26 = bf16[256,2048]{1,0:T(8,128)(2,1)} fusion(bf16[256,8192]{1,0:T(8,128)(2,1)} %all-gather.3.cloned.1.call-done, bf16[2048,16384]{1,0:T(8,128)(2,1)} %constant_dynamic-update-slice_fusion, s32[]{:T(128)S(6)} %select_n.73, bf16[256,2048]{1,0:T(8,128)(2,1)S(1)} %copy-done.9, f32[2048]{0:T(1024)S(1)} %bitcast.94), kind=kOutput, calls=%fused_computation.27 | convolution fusion | flops 8592556032 | bytes 39854084 | tf_op jit(solution)/shard_map/dot_general | solution.py:84
  (60 shorter events, 1.9 us)
Async XLA Ops:
  6.5 96.8 %collective-permute-start = (bf16[2048,1024]{1,0:T(8,128)(2,1)}, bf16[2048,1024]{1,0:T(8,128)(2,1)S(1)}, u32[]{:S(2)}, u32[]{:S(2)}) collective-permute-start(bf16[2048,1024]{1,0:T(8,128)(2,1)} %bitcast.83), channel_id=1, source_target_pairs={{0,4},{4,8},{8,12},{12,16},{16,20},{20,24},{24,28},{28,0},{1,5},{5... | collective-permute-start | bytes 12582920 | tf_op jit(solution)/shard_map/ppermute | solution.py:79
  103.3 2.0 copy-start.1
  105.3 94.5 %collective-permute-start.1 = (bf16[2048,1024]{1,0:T(8,128)(2,1)S(1)}, bf16[2048,1024]{1,0:T(8,128)(2,1)S(1)}, u32[]{:S(2)}, u32[]{:S(2)}) collective-permute-start(bf16[2048,1024]{1,0:T(8,128)(2,1)S(1)} %collective-permute-done), channel_id=1, source_target_pairs={{0,4},{4,8},{8,12},{12,16},{16,20},{20,24},{24,28},{28,0},{1,5},{5... | collective-permute-start | bytes 12582920 | tf_op jit(solution)/shard_map/ppermute | solution.py:79
  199.7 2.0 copy-start.3
  201.7 93.5 %collective-permute-start.2 = (bf16[2048,1024]{1,0:T(8,128)(2,1)S(1)}, bf16[2048,1024]{1,0:T(8,128)(2,1)S(1)}, u32[]{:S(2)}, u32[]{:S(2)}) collective-permute-start(bf16[2048,1024]{1,0:T(8,128)(2,1)S(1)} %collective-permute-done.1), channel_id=1, source_target_pairs={{0,4},{4,8},{8,12},{12,16},{16,20},{20,24},{24,28},{28,0},{1,5},{5... | collective-permute-start | bytes 12582920 | tf_op jit(solution)/shard_map/ppermute | solution.py:79
  295.2 2.0 copy-start.5
  297.2 92.6 %collective-permute-start.3 = (bf16[2048,1024]{1,0:T(8,128)(2,1)S(1)}, bf16[2048,1024]{1,0:T(8,128)(2,1)S(1)}, u32[]{:S(2)}, u32[]{:S(2)}) collective-permute-start(bf16[2048,1024]{1,0:T(8,128)(2,1)S(1)} %collective-permute-done.2), channel_id=1, source_target_pairs={{0,4},{4,8},{8,12},{12,16},{16,20},{20,24},{24,28},{28,0},{1,5},{5... | collective-permute-start | bytes 12582920 | tf_op jit(solution)/shard_map/ppermute | solution.py:79
  389.8 2.0 copy-start.7
  391.8 91.8 %collective-permute-start.4 = (bf16[2048,1024]{1,0:T(8,128)(2,1)S(1)}, bf16[2048,1024]{1,0:T(8,128)(2,1)}, u32[]{:S(2)}, u32[]{:S(2)}) collective-permute-start(bf16[2048,1024]{1,0:T(8,128)(2,1)S(1)} %collective-permute-done.3), channel_id=1, source_target_pairs={{0,4},{4,8},{8,12},{12,16},{16,20},{20,24},{24,28},{28,0},{1,5},{5... | collective-permute-start | bytes 12582920 | tf_op jit(solution)/shard_map/ppermute | solution.py:79
  483.6 91.1 %collective-permute-start.5 = (bf16[2048,1024]{1,0:T(8,128)(2,1)}, bf16[2048,1024]{1,0:T(8,128)(2,1)}, u32[]{:S(2)}, u32[]{:S(2)}) collective-permute-start(bf16[2048,1024]{1,0:T(8,128)(2,1)} %collective-permute-done.4), channel_id=1, source_target_pairs={{0,4},{4,8},{8,12},{12,16},{16,20},{20,24},{24,28},{28,0},{1,5},{5... | collective-permute-start | bytes 12582920 | tf_op jit(solution)/shard_map/ppermute | solution.py:79
  484.9 95.2 %all-to-all-start.1 = ((s32[8,1,1]{2,1,0:T(1,128)}), s32[8,1,1]{2,1,0:T(1,128)S(1)}, u32[]{:S(2)}, u32[]{:S(2)}) async-start(s32[8,1,1]{2,1,0:T(1,128)} %copy.32), calls=%async_computation.1 | async-start | bytes 8192 | tf_op jit(solution)/shard_map/all_to_all | solution.py:58
  493.3 12.4 %copy-start.10 = (s32[1,8]{1,0:T(1,128)S(1)}, s32[1,8]{1,0:T(1,128)}, u32[]{:S(2)}) copy-start(s32[1,8]{1,0:T(1,128)} %param.9) | copy-start | bytes 100
  574.7 115.7 %collective-permute-start.6 = (bf16[2048,1024]{1,0:T(8,128)(2,1)}, bf16[2048,1024]{1,0:T(8,128)(2,1)}, u32[]{:S(2)}, u32[]{:S(2)}) collective-permute-start(bf16[2048,1024]{1,0:T(8,128)(2,1)} %collective-permute-done.5), channel_id=1, source_target_pairs={{0,4},{4,8},{8,12},{12,16},{16,20},{20,24},{24,28},{28,0},{1,5},{5... | collective-permute-start | bytes 12582920 | tf_op jit(solution)/shard_map/ppermute | solution.py:79
  580.1 107.9 %all-to-all-start = ((bf16[8,48,2048]{2,1,0:T(8,128)(2,1)}), bf16[8,48,2048]{2,1,0:T(8,128)(2,1)S(1)}, u32[]{:S(2)}, u32[]{:S(2)}) async-start(bf16[8,48,2048]{2,1,0:T(8,128)(2,1)} %broadcast_select_fusion), calls=%async_computation | async-start | bytes 3145728 | tf_op jit(solution)/shard_map/all_to_all | solution.py:57
  586.1 156.4 %all-gather.3.cloned.1.call-start = ((), (), s32[]{:S(2)}) async-start(), calls=%async_computation.2 | async-start | bytes 5242880 | tf_op jit(solution)/shard_map/all_gather | solution.py:73
  694.9 9.5 %copy-start.8 = (bf16[2048,1024]{1,0:T(8,128)(2,1)S(1)}, bf16[2048,1024]{1,0:T(8,128)(2,1)}, u32[]{:S(2)}) copy-start(bf16[2048,1024]{1,0:T(8,128)(2,1)} %copy-done.7) | copy-start | bytes 12582916
  699.7 7.4 copy-start.6
  704.4 5.3 copy-start.4
  707.0 5.2 copy-start.2
  709.6 5.0 copy-start
  737.8 4.7 copy-start.9
  737.8 4.7 copy-start.11
Sparse Core Ops, SparseCore 0:
  690.5 41.2 all-gather.2
